TPU v7x, 256 devices: a whole 4x4x8 slice. The times are simulated.
256 devices in a mesh: outer: 32 (over z, x), inner: 8 (over y, core).
Axes of the slice: x: 4, y: 4, z: 8, core: 2. Of those that a mesh axis runs over, the one named last changes fastest.
Arguments:
- queries: bfloat16 [32768, 2048], P(('outer', 'inner')), may hold values from -5 to 5
- key_rows: bfloat16 [32768, 2048], P(('outer', 'inner')), may hold values from -5 to 5
- value_rows: bfloat16 [32768, 2048], P(('outer', 'inner')), may hold values from -6 to 6
- out_grad: bfloat16 [32768, 2048], P(('outer', 'inner')), may hold values from -6 to 6
- log_gate: float32 [16, 32768], P(None, ('outer', 'inner')), may hold values from -1 to 0
Outputs:
- mixed_out: bfloat16 [32768, 2048], P(('outer', 'inner'))
- query_grad: bfloat16 [32768, 2048], P(('outer', 'inner'))
- key_grad: bfloat16 [32768, 2048], P(('outer', 'inner'))
- value_grad: bfloat16 [32768, 2048], P(('outer', 'inner'))
All inputs are finite; a program needn't handle non-finite values.
Results may differ from a plain program's by a relative error of at most 0.007.
Values may be sent and summed in bfloat16 or wider, within the bound.
No kernel may reach another device: no remote copies, remote signals or barrier semaphores. Data moves between devices by JAX's collectives and lax.ppermute only.
A program may use at most 256 MiB of HBM per device.

v0:
```python
import jax
import jax.numpy as jnp
from jax import lax
from jax.sharding import PartitionSpec as P

W = 64


def from_behind(value, axis, steps):
    count = lax.axis_size(axis)
    first, last = (max(0, -steps), min(count, count - steps))
    return lax.ppermute(value, axis, [(source, source + steps) for source in range(first, last)])


def carried_in(part, axis, combine, identity, reverse):
    count = lax.axis_size(axis)
    place = lax.axis_index(axis)
    ahead = count - 1 - place if reverse else place
    gathered = jax.tree.map(lambda a: lax.all_gather(a, axis), part)
    state = jax.tree.map(lambda a, e: jnp.zeros_like(a) + jnp.asarray(e, a.dtype), part, identity)

    def one(hop, state):
        source = count - 1 - hop if reverse else hop
        return combine(
            state, jax.tree.map(lambda a: lax.dynamic_index_in_dim(a, source, 0, False), gathered)
        )

    return lax.fori_loop(0, ahead, one, state)


def low_product(form, left, right):
    return jnp.einsum(form, left, right, preferred_element_type=jnp.float32)


def high_product(form, left, right):
    return jnp.einsum(form, left, right, precision=lax.Precision.HIGHEST)


def local_states(query_blk, key_blk, value_blk, grad_blk, gate_rows):
    cumul_gate = jnp.cumsum(gate_rows, axis=1)
    last_cumul = cumul_gate[:, -1:]
    block_decay = jnp.exp(cumul_gate[:, -1])
    tail_weight = jnp.exp(last_cumul - cumul_gate).T
    head_weight = jnp.exp(cumul_gate).T
    state_local = high_product(
        "thf,the->hfe",
        key_blk.astype(jnp.float32) * tail_weight[:, :, None],
        value_blk.astype(jnp.float32),
    )
    grad_local = high_product(
        "thf,the->hfe",
        query_blk.astype(jnp.float32) * head_weight[:, :, None],
        grad_blk.astype(jnp.float32),
    )
    return (block_decay, state_local, grad_local)


def block_terms(
    query_blk,
    key_blk,
    value_blk,
    grad_blk,
    gate_rows,
    state_in,
    grad_after,
    key_halo,
    value_halo,
    halo_live,
    lin_scale,
):
    row_count = query_blk.shape[0]
    halo_rows = key_halo.shape[0]
    head_size = query_blk.shape[2]
    cumul_gate = jnp.cumsum(gate_rows, axis=1)
    last_cumul = cumul_gate[:, -1:]
    head_weight = jnp.exp(cumul_gate).T
    tail_weight = jnp.exp(last_cumul - cumul_gate).T
    query_pos = jnp.arange(row_count)[:, None]
    key_pos = jnp.arange(row_count)[None, :]
    causal_mask = (key_pos <= query_pos)[None]
    gap_logs = cumul_gate[:, :, None] - cumul_gate[:, None, :]
    decay_grid = jnp.where(causal_mask, jnp.exp(jnp.where(causal_mask, gap_logs, 0.0)), 0.0)
    lin_weight = (low_product("thf,shf->hts", query_blk, key_blk) * decay_grid).astype(jnp.bfloat16)
    query_decayed = query_blk.astype(jnp.float32) * head_weight[:, :, None]
    lin_out = low_product("hts,she->the", lin_weight, value_blk) + high_product(
        "thf,hfe->the", query_decayed, state_in
    )
    ext_keys = jnp.concatenate([key_halo, key_blk], axis=0)
    ext_values = jnp.concatenate([value_halo, value_blk], axis=0)
    ext_pos = jnp.arange(row_count + halo_rows)[None, :]
    in_band = (
        (ext_pos > query_pos)
        & (ext_pos <= query_pos + halo_rows)
        & ((ext_pos >= halo_rows) | halo_live)
    )[None]
    logits = low_product("thf,jhf->htj", query_blk, ext_keys) * head_size ** (-0.5)
    masked_logits = jnp.where(in_band, logits, -jnp.inf)
    row_max = jnp.max(masked_logits, axis=2, keepdims=True)
    expo_terms = jnp.exp(masked_logits - row_max)
    win_prob = expo_terms / jnp.sum(expo_terms, axis=2, keepdims=True)
    prob_low = win_prob.astype(jnp.bfloat16)
    win_out = low_product("htj,jhe->the", prob_low, ext_values)
    output = (lin_scale * lin_out + win_out).astype(jnp.bfloat16)
    grad_weight = (low_product("the,she->hts", grad_blk, value_blk) * decay_grid).astype(
        jnp.bfloat16
    )
    grad_decayed = grad_blk.astype(jnp.float32) * head_weight[:, :, None]
    query_lin = low_product("hts,shf->thf", grad_weight, key_blk) + high_product(
        "the,hfe->thf", grad_decayed, state_in
    )
    value_tail = value_blk.astype(jnp.float32) * tail_weight[:, :, None]
    key_tail = key_blk.astype(jnp.float32) * tail_weight[:, :, None]
    key_lin = low_product("hts,thf->shf", grad_weight, query_blk) + high_product(
        "she,hfe->shf", value_tail, grad_after
    )
    value_lin = low_product("hts,the->she", lin_weight, grad_blk) + high_product(
        "shf,hfe->she", key_tail, grad_after
    )
    prob_grad = low_product("the,jhe->htj", grad_blk, ext_values)
    row_delta = jnp.sum(win_prob * prob_grad, axis=2, keepdims=True)
    logit_grad = (win_prob * (prob_grad - row_delta) * head_size ** (-0.5)).astype(jnp.bfloat16)
    query_win = low_product("htj,jhf->thf", logit_grad, ext_keys)
    key_ext = low_product("htj,thf->jhf", logit_grad, query_blk)
    value_ext = low_product("htj,the->jhe", prob_low, grad_blk)
    query_grad = (lin_scale * query_lin + query_win).astype(jnp.bfloat16)
    key_local = lin_scale * key_lin + key_ext[halo_rows:]
    value_local = lin_scale * value_lin + value_ext[halo_rows:]
    return (output, query_grad, key_local, value_local, key_ext[:halo_rows], value_ext[:halo_rows])


def forward_merge(earlier_part, later_part):
    return (
        earlier_part[0] * later_part[0],
        later_part[0][:, None, None] * earlier_part[1] + later_part[1],
    )


def backward_merge(earlier_part, later_part):
    return (
        earlier_part[0] * later_part[0],
        later_part[1] + later_part[0][:, None, None] * earlier_part[1],
    )


def run_forward(running, element):
    return (forward_merge(running, element), running)


def run_backward(running, element):
    return (backward_merge(running, element), running)


def select_mine(bundle, inner_pos):
    return tuple(
        (lax.dynamic_index_in_dim(member, inner_pos, 0, keepdims=False) for member in bundle)
    )


def per_device(queries, key_rows, value_rows, out_grad, log_gate):
    row_count = queries.shape[0]
    head_count = log_gate.shape[0]
    head_size = queries.shape[1] // head_count
    devices = lax.axis_size("outer") * lax.axis_size("inner")
    lin_scale = (head_size * row_count * devices) ** (-0.5)
    block_shape = (row_count, head_count, head_size)
    query_blk = queries.reshape(block_shape)
    key_blk = key_rows.reshape(block_shape)
    value_blk = value_rows.reshape(block_shape)
    grad_blk = out_grad.reshape(block_shape)
    block_decay, state_local, grad_local = local_states(
        query_blk, key_blk, value_blk, grad_blk, log_gate
    )
    key_halo, value_halo = from_behind((key_blk[-W:], value_blk[-W:]), ("outer", "inner"), 1)
    position = lax.axis_index("outer") * lax.axis_size("inner") + lax.axis_index("inner")
    identity_pair = (
        jnp.ones((head_count,), jnp.float32),
        jnp.zeros((head_count, head_size, head_size), jnp.float32),
    )
    gathered = (
        lax.all_gather(block_decay[None], "inner", axis=0, tiled=True),
        lax.all_gather(state_local[None], "inner", axis=0, tiled=True),
        lax.all_gather(grad_local[None], "inner", axis=0, tiled=True),
    )
    group_decay, group_state, group_grad = gathered
    total_forward, before_forward = lax.scan(run_forward, identity_pair, (group_decay, group_state))
    total_backward, after_backward = lax.scan(
        run_backward, identity_pair, (group_decay, group_grad), reverse=True
    )
    inner_pos = lax.axis_index("inner")
    mine_forward = select_mine(before_forward, inner_pos)
    mine_backward = select_mine(after_backward, inner_pos)
    outer_forward = carried_in(total_forward, "outer", forward_merge, identity_pair, False)
    outer_backward = carried_in(total_backward, "outer", backward_merge, identity_pair, True)
    forward_pair = forward_merge(outer_forward, mine_forward)
    backward_pair = backward_merge(outer_backward, mine_backward)
    output, query_grad, key_local, value_local, key_back, value_back = block_terms(
        query_blk,
        key_blk,
        value_blk,
        grad_blk,
        log_gate,
        forward_pair[1],
        backward_pair[1],
        key_halo,
        value_halo,
        position > 0,
        lin_scale,
    )
    key_return, value_return = (
        from_behind(key_back.astype(jnp.bfloat16), ("outer", "inner"), -1).astype(key_back.dtype),
        from_behind(value_back.astype(jnp.bfloat16), ("outer", "inner"), -1).astype(
            value_back.dtype
        ),
    )
    key_grad = key_local.at[-W:].add(key_return).astype(jnp.bfloat16)
    value_grad = value_local.at[-W:].add(value_return).astype(jnp.bfloat16)
    flat_shape = (row_count, head_count * head_size)
    return (
        output.reshape(flat_shape),
        query_grad.reshape(flat_shape),
        key_grad.reshape(flat_shape),
        value_grad.reshape(flat_shape),
    )


def solution(mesh):
    placed = (
        P(("outer", "inner"), None),
        P(("outer", "inner"), None),
        P(("outer", "inner"), None),
        P(("outer", "inner"), None),
        P(None, ("outer", "inner")),
    )
    return jax.shard_map(
        per_device,
        mesh=mesh,
        in_specs=placed,
        out_specs=(
            P(("outer", "inner"), None),
            P(("outer", "inner"), None),
            P(("outer", "inner"), None),
            P(("outer", "inner"), None),
        ),
        check_vma=False,
    )
```

profile of v0, /device:TPU:230, one launch (start us, length us, event | category | flops | bytes accessed | tf_op | source)
XLA Modules:
  0.0 660.7 jit_solution(8102679605573216670)
XLA Ops:
  11.1 2.2 fusion.33
  14.6 2.2 fusion.34
  18.4 15.5 %all-reduce = f32[128]{0:T(128)S(1)} all-reduce(f32[128]{0:T(128)S(1)} %dynamic-update-slice.6), channel_id=2, replica_groups=mesh['outer'=32,'inner'=8] {'inner'}, use_global_device_ids=true, to_apply=%add | all-reduce | flops 128 | bytes 1024
  34.0 32.2 %all-gather.16.cloned.1.call-done = f32[128,128,128]{2,1,0:T(8,128)} async-done(((f32[16,128,128]{2,1,0:T(8,128)}), f32[128,128,128]{2,1,0:T(8,128)}) %all-gather.16.cloned.1.call-update) | async-done | bytes 8388624 | tf_op jit(solution)/shard_map/all_gather | solution.py:182
  66.1 4.4 broadcast.104.clone.1
  70.5 21.0 %while.69 = (s32[]{:T(128)}, f32[16]{0:T(128)S(1)}, f32[16,128,128]{2,1,0:T(8,128)S(1)}, f32[8,16]{1,0:T(8,128)S(1)}, f32[8,16,128,128]{3,2,1,0:T(8,128)}, /*ind...) while((s32[]{:T(128)}, f32[16]{0:T(128)S(1)}, ...), condition=%wide.region_9.10_spmd.clone, body=%wide.region_8.9_spmd.clone.sunk | while | flops 1048612 | bytes 5243533 | solution.py:186
  79.3 1.5 bitcast_add_fusion.17
  82.1 1.6 bitcast_add_fusion.17
  92.6 27.8 %all-gather.12.cloned.1.call-done = f32[128,128,128]{2,1,0:T(8,128)} async-done(((f32[16,128,128]{2,1,0:T(8,128)}), f32[128,128,128]{2,1,0:T(8,128)}) %all-gather.12.cloned.1.call-update) | async-done | bytes 8388624 | tf_op jit(solution)/shard_map/all_gather | solution.py:181
  120.4 4.3 broadcast.104.clone
  124.7 20.6 %while.68 = (s32[]{:T(128)}, f32[16]{0:T(128)S(1)}, f32[16,128,128]{2,1,0:T(8,128)S(1)}, f32[8,16]{1,0:T(8,128)S(1)}, f32[8,16,128,128]{3,2,1,0:T(8,128)}, /*ind...) while((s32[]{:T(128)}, f32[16]{0:T(128)S(1)}, ...), condition=%wide.region_2.3_spmd.clone, body=%wide.region_1.2_spmd.clone.sunk | while | flops 1048611 | bytes 5244021 | solution.py:185
  136.0 1.5 bitcast_add_fusion.16
  146.3 1.7 copy_bitcast_fusion
  148.0 2.2 collective-permute-start.1
  151.2 2.5 collective-permute-start
  157.0 1.5 convolution_bitcast_fusion.7
  158.5 1.5 convolution_bitcast_fusion.9
  160.0 2.6 collective-permute-done.1
  162.6 2.7 fusion.70
  165.3 3.3 convolution_bitcast_fusion
  168.6 2.2 slice.107
  170.8 2.5 collective-permute-start.3
  173.3 2.5 fusion.44
  175.8 4.8 convolution_bitcast_fusion.1
  180.7 2.1 slice.108
  182.8 2.1 collective-permute-start.2
  185.4 72.2 %all-reduce.3 = (f32[512]{0:T(512)S(1)}, f32[512]{0:T(512)S(1)}) all-reduce(f32[512]{0:T(512)S(1)} %dynamic-update-slice.7, f32[512]{0:T(512)S(1)} %dynamic-update-slice.8), channel_id=4, replica_groups=mesh['outer'=32,'inner'=8] {'outer'}, use_global_device_ids=true, to_apply=%add.1 | all-reduce | flops 1024 | bytes 8192
  257.7 100.4 %all-gather.18.cloned.1.call-done = f32[512,128,128]{2,1,0:T(8,128)} async-done(((f32[16,128,128]{2,1,0:T(8,128)}), f32[512,128,128]{2,1,0:T(8,128)}) %all-gather.18.cloned.1.call-update) | async-done | bytes 33554448 | tf_op jit(solution)/shard_map/all_gather | solution.py:19
  358.5 3.3 convolution_bitcast_fusion.4
  363.3 2.4 slice_add_fusion
  365.6 7.0 %scatter-add.9 = f32[128,16,128]{0,2,1:T(8,128)} dynamic-update-slice(f32[128,16,128]{0,2,1:T(8,128)} %copy-done.2, f32[64,16,128]{0,2,1:T(8,128)} %slice_add_fusion, s32[]{:T(128)} %constant.187.clone.1, s32[]{:T(128)} %constant.180.clone.1, s32[]{:T(128)} %constant.180.clone.1) | dynamic-update-slice | bytes 1048580 | tf_op jit(solution)/shard_map/scatter-add | solution.py:216
  375.1 2.8 convolution_bitcast_fusion.5
  379.7 5.1 scatter-add.6
  385.9 204.5 %all-gather.14.cloned.1.call-done = f32[512,128,128]{2,1,0:T(8,128)} async-done(((f32[16,128,128]{2,1,0:T(8,128)}), f32[512,128,128]{2,1,0:T(8,128)}) %all-gather.14.cloned.1.call-update) | async-done | bytes 33554448 | tf_op jit(solution)/shard_map/all_gather | solution.py:19
  590.6 46.6 %while.66 = (s32[]{:T(128)}, f32[16,128,128]{2,1,0:T(8,128)S(1)}, s32[]{:T(128)}, f32[32,16]{1,0:T(8,128)S(1)}, f32[32,16,128,128]{3,2,1,0:T(8,128)}, /*index=5*/s32[]{:T(128)}, s32[]{:T(128)}, s32[]{:T(128)}) while((s32[]{:T(128)}, f32[16,128,128]{2,1,0:T(8,128)S(1)}, s32[]{:T(128)}, f32[32,16]{1,0:T(8,128)S(1)}, ...), condition=%wide.region_4.5_spmd, body=%wide.region_3.4_spmd.sunk | while | flops 524293 | bytes 3146047 | solution.py:28
  590.6 1.5 bitcast_add_fusion.14
  595.2 1.4 bitcast_add_fusion.14
  598.2 1.4 bitcast_add_fusion.14
  602.7 1.4 bitcast_add_fusion.14
  607.2 1.4 bitcast_add_fusion.14
  610.2 1.4 bitcast_add_fusion.14
  611.7 1.4 bitcast_add_fusion.14
  614.7 1.4 bitcast_add_fusion.14
  619.2 1.4 bitcast_add_fusion.14
  637.1 3.6 fusion.20
  640.7 4.3 fusion.26
  646.5 4.2 fusion.22
  650.7 2.5 fusion.25
  (208 shorter events, 90.6 us)
Async XLA Ops:
  7.2 59.0 %all-gather.16.cloned.1.call-start = ((), (), s32[]{:S(2)}) async-start(), calls=%async_computation.2 | async-start | bytes 9437184 | tf_op jit(solution)/shard_map/all_gather | solution.py:182
  11.1 2.3 copy-start.11
  13.3 1.0 copy-start.12
  13.3 107.1 %all-gather.12.cloned.1.call-start = ((), (), s32[]{:S(2)}) async-start(), calls=%async_computation | async-start | bytes 9437184 | tf_op jit(solution)/shard_map/all_gather | solution.py:181
  14.6 2.3 copy-start.17
  16.8 341.3 %all-gather.18.cloned.1.call-start = ((), (), s32[]{:S(2)}) async-start(), calls=%async_computation.3 | async-start | bytes 34603008 | tf_op jit(solution)/shard_map/all_gather | solution.py:19
  91.5 1.0 copy-start
  92.5 498.0 %all-gather.14.cloned.1.call-start = ((), (), s32[]{:S(2)}) async-start(), calls=%async_computation.1 | async-start | bytes 34603008 | tf_op jit(solution)/shard_map/all_gather | solution.py:19
  145.3 1.0 copy-start.1
  146.3 8.1 %copy-start.16 = (u32[256]{0:T(256)S(1)}, u32[256]{0:T(256)}, u32[]{:S(2)}) copy-start(u32[256]{0:T(256)} %constant.203) | copy-start | bytes 3076
  148.0 14.6 %collective-permute-start.1 = (bf16[64,16,128]{2,0,1:T(8,128)(2,1)}, bf16[64,16,128]{2,0,1:T(8,128)(2,1)}, u32[]{:S(2)}, u32[]{:S(2)}) collective-permute-start(bf16[64,16,128]{2,0,1:T(8,128)(2,1)} %copy_bitcast_fusion), channel_id=1, source_target_pairs={{0,1},{1,2},{2,3},{3,4},{4,5},{5,6},{6,7},{7,8},{8,9},{9,10},{10,1... | collective-permute-start | bytes 786440 | tf_op jit(solution)/shard_map/ppermute | solution.py:12
  151.2 22.1 %collective-permute-start = (bf16[64,16,128]{2,0,1:T(8,128)(2,1)S(1)}, bf16[64,16,128]{2,0,1:T(8,128)(2,1)}, u32[]{:S(2)}, u32[]{:S(2)}) collective-permute-start(bf16[64,16,128]{2,0,1:T(8,128)(2,1)S(1)} %copy_bitcast_fusion.1), channel_id=1, source_target_pairs={{0,1},{1,2},{2,3},{3,4},{4,5},{5,6},{6,7},{7,8},{8,9},{9,10},{10,1... | collective-permute-start | bytes 786440 | tf_op jit(solution)/shard_map/ppermute | solution.py:12
  154.0 11.2 %copy-start.15 = (bf16[128,16,128]{2,0,1:T(8,128)(2,1)}, bf16[128,16,128]{2,0,1:T(8,128)(2,1)S(1)}, u32[]{:S(2)}) copy-start(bf16[128,16,128]{2,0,1:T(8,128)(2,1)S(1)} %copy.84) | copy-start | bytes 1572868
  154.3 19.0 %copy-start.5 = (bf16[128,16,128]{2,0,1:T(8,128)(2,1)}, bf16[128,16,128]{2,0,1:T(8,128)(2,1)S(1)}, u32[]{:S(2)}) copy-start(bf16[128,16,128]{2,0,1:T(8,128)(2,1)S(1)} %copy.82) | copy-start | bytes 1572868
  156.4 2.1 copy-start.9
  157.0 3.0 copy-start.7
  170.8 191.5 %collective-permute-start.3 = (bf16[64,16,128]{0,2,1:T(8,128)(2,1)}, bf16[64,16,128]{0,2,1:T(8,128)(2,1)}, u32[]{:S(2)}, u32[]{:S(2)}) collective-permute-start(bf16[64,16,128]{0,2,1:T(8,128)(2,1)} %slice.107), channel_id=1, source_target_pairs={{1,0},{2,1},{3,2},{4,3},{5,4},{6,5},{7,6},{8,7},{9,8},{10,9},{11,1... | collective-permute-start | bytes 786440 | tf_op jit(solution)/shard_map/ppermute | solution.py:12
  182.8 195.6 %collective-permute-start.2 = (bf16[64,16,128]{0,2,1:T(8,128)(2,1)}, bf16[64,16,128]{0,2,1:T(8,128)(2,1)}, u32[]{:S(2)}, u32[]{:S(2)}) collective-permute-start(bf16[64,16,128]{0,2,1:T(8,128)(2,1)} %slice.108), channel_id=1, source_target_pairs={{1,0},{2,1},{3,2},{4,3},{5,4},{6,5},{7,6},{8,7},{9,8},{10,9},{11,1... | collective-permute-start | bytes 786440 | tf_op jit(solution)/shard_map/ppermute | solution.py:12
  358.5 3.4 copy-start.10
  358.5 3.4 copy-start.14
  362.3 1.0 copy-start.2
  375.1 2.8 copy-start.8
  375.1 2.8 copy-start.13
  590.6 46.6 %copy-start.4 = (f32[128,16,128]{0,2,1:T(8,128)S(1)}, f32[128,16,128]{0,2,1:T(8,128)}, u32[]{:S(2)}) copy-start(f32[128,16,128]{0,2,1:T(8,128)} %convolution_bitcast_fusion.7) | copy-start | bytes 3145732
  645.0 1.4 copy-start.3
  646.5 4.2 copy-start.6
Sparse Core Ops, SparseCore 0:
  13.5 52.6 all-gather.15
  68.0 52.3 all-gather.11
  123.0 235.1 all-gather.17
  360.6 229.8 all-gather.13
where the time goes:
time: 664 us; the launch traced here: 661 us
  waiting for transfers between devices  368 us (55%)
  other arithmetic  92.1 us (14%)
  blocking collectives  87.6 us (13%)
  matrix products  43.3 us (7%)
  local copies, waits for them, and re-layouts  43.1 us (6%)
  between operations  15.6 us (2%)
  starting transfers between devices  9.56 us (1%)
    all_gather x2, waiting for transfers between devices, carried_in(): gathered = jax.tree.map(lambda a: lax.all_gather(a, axis), part)  305 us
    unnamed x2, blocking collectives  87.6 us
    add x39, other arithmetic, forward_merge(): later_part[0][:, None, None] * earlier_part[1] + later_part[1]  56.4 us
    all_gather x1, waiting for transfers between devices, per_device(): lax.all_gather(grad_local[None], 'inner', axis=0, tiled=True)  32.2 us
    all_gather x1, waiting for transfers between devices, per_device(): lax.all_gather(state_local[None], 'inner', axis=0, tiled=True)  27.8 us
    dot_general x11, matrix products, low_product(): return jnp.einsum(form, left, right, preferred_element_type=jnp.float32)  22.3 us
    dot_general x6, matrix products, high_product(): return jnp.einsum(form, left, right, precision=lax.Precision.HIGHEST)  18.3 us
    dynamic_update_slice x16, other arithmetic, per_device(): lax.scan(run_forward, identity_pair, (group_decay, group_state))  17.3 us
  transfers between devices with their start and end apart: 8, of which 5 were waited for; matrix products, arithmetic and copies ran while one was open for 16% of the time, Pallas kernels for 0%

commit v1 on v0

--- a/solution.py
+++ b/solution.py
@@ -4,6 +4,27 @@
 from jax.sharding import PartitionSpec as P
 
 W = 64
+
+
+def ring_gather(value, axis, dim):
+    count, position, extent = (lax.axis_size(axis), lax.axis_index(axis), value.shape[dim])
+    right = [(i, (i + 1) % count) for i in range(count)]
+    backward = [(i, (i - 1) % count) for i in range(count)]
+    out = jnp.zeros((*value.shape[:dim], count * extent, *value.shape[dim + 1 :]), value.dtype)
+    out = lax.dynamic_update_slice_in_dim(out, value, position * extent, axis=dim)
+    from_left = from_right = value
+    middle = count // 2
+    for lap in range(1, middle + 1):
+        from_left = lax.ppermute(from_left, axis, right)
+        out = lax.dynamic_update_slice_in_dim(
+            out, from_left, (position - lap) % count * extent, axis=dim
+        )
+        if lap < count - middle:
+            from_right = lax.ppermute(from_right, axis, backward)
+            out = lax.dynamic_update_slice_in_dim(
+                out, from_right, (position + lap) % count * extent, axis=dim
+            )
+    return out
 
 
 def from_behind(value, axis, steps):
@@ -178,7 +199,7 @@
     )
     gathered = (
         lax.all_gather(block_decay[None], "inner", axis=0, tiled=True),
-        lax.all_gather(state_local[None], "inner", axis=0, tiled=True),
+        ring_gather(state_local[None], "inner", 0),
         lax.all_gather(grad_local[None], "inner", axis=0, tiled=True),
     )
     group_decay, group_state, group_grad = gathered

time: 664 us -> 718 us (1.081)
  the two profiles are of different devices: /device:TPU:230 before, /device:TPU:1 now
where the time goes in v1:
time: 718 us; the launch traced here: 715 us
  waiting for transfers between devices  376 us (52%)
  blocking collectives  91.3 us (13%)
  other arithmetic  90.8 us (13%)
  local copies, waits for them, and re-layouts  62.3 us (9%)
  matrix products  47.6 us (7%)
  starting transfers between devices  29.4 us (4%)
  between operations  15.4 us (2%)
    all_gather x2, waiting for transfers between devices, carried_in(): gathered = jax.tree.map(lambda a: lax.all_gather(a, axis), part)  321 us
    unnamed x2, blocking collectives  91.3 us
    add x39, other arithmetic, backward_merge(): later_part[1] + later_part[0][:, None, None] * earlier_part[1]  56.5 us
    ppermute x4, waiting for transfers between devices, ring_gather(): from_left = lax.ppermute(from_left, axis, right)  54.7 us
    dot_general x11, matrix products, low_product(): return jnp.einsum(form, left, right, preferred_element_type=jnp.float32)  25 us
    dot_general x6, matrix products, high_product(): return jnp.einsum(form, left, right, precision=lax.Precision.HIGHEST)  19.9 us
    dynamic_update_slice x16, other arithmetic, per_device(): lax.scan(run_forward, identity_pair, (group_decay, group_state))  17.3 us
  transfers between devices with their start and end apart: 14, of which 6 were waited for; matrix products, arithmetic and copies ran while one was open for 26% of the time, Pallas kernels for 0%

profile of v1, /device:TPU:1, one launch (start us, length us, event | category | flops | bytes accessed | tf_op | source)
XLA Modules:
  0.0 714.9 jit_solution(8747434265890142447)
XLA Ops:
  11.1 2.2 fusion.33
  14.6 4.3 broadcast.111.clone.1
  18.9 2.2 constant_dynamic-update-slice_fusion.7
  21.1 2.7 collective-permute-start
  24.4 20.0 %collective-permute-done = f32[1,16,128,128]{3,2,1,0:T(8,128)S(1)} collective-permute-done((f32[1,16,128,128]{3,2,1,0:T(8,128)S(1)}, f32[1,16,128,128]{3,2,1,0:T(8,128)S(1)}, u32[]{:S(2)}, u32[]{:S(2)}) %collective-permute-start) | collective-permute-done | bytes 1048608 | tf_op jit(solution)/shard_map/ppermute | solution.py:18
  45.4 2.5 collective-permute-start.2
  47.9 6.9 collective-permute-start.3
  54.8 25.7 %collective-permute-done.2 = f32[1,16,128,128]{3,2,1,0:T(8,128)S(1)} collective-permute-done((f32[1,16,128,128]{3,2,1,0:T(8,128)S(1)}, f32[1,16,128,128]{3,2,1,0:T(8,128)S(1)}, u32[]{:S(2)}, u32[]{:S(2)}) %collective-permute-start.2) | collective-permute-done | bytes 1048608 | tf_op jit(solution)/shard_map/ppermute | solution.py:18
  80.5 2.5 collective-permute-start.4
  83.2 2.5 collective-permute-start.5
  85.8 8.9 %collective-permute-done.4 = f32[1,16,128,128]{3,2,1,0:T(8,128)} collective-permute-done((f32[1,16,128,128]{3,2,1,0:T(8,128)S(1)}, f32[1,16,128,128]{3,2,1,0:T(8,128)}, u32[]{:S(2)}, u32[]{:S(2)}) %collective-permute-start.4) | collective-permute-done | bytes 1048608 | tf_op jit(solution)/shard_map/ppermute | solution.py:18
  94.7 2.6 collective-permute-start.6
  98.8 23.5 %all-reduce = f32[128]{0:T(128)S(1)} all-reduce(f32[128]{0:T(128)S(1)} %dynamic-update-slice.6), channel_id=2, replica_groups=mesh['outer'=32,'inner'=8] {'inner'}, use_global_device_ids=true, to_apply=%add | all-reduce | flops 128 | bytes 1024
  122.4 2.5 constant_dynamic-update-slice_fusion.6
  127.5 2.3 constant_dynamic-update-slice_fusion.3
  129.9 2.3 constant_dynamic-update-slice_fusion.2
  132.2 2.4 constant_dynamic-update-slice_fusion.1
  134.5 2.3 constant_dynamic-update-slice_fusion
  136.8 4.3 broadcast.111.clone
  141.1 20.5 %while.68 = (s32[]{:T(128)}, f32[16]{0:T(128)S(1)}, f32[16,128,128]{2,1,0:T(8,128)S(1)}, f32[8,16]{1,0:T(8,128)S(1)}, f32[8,16,128,128]{3,2,1,0:T(8,128)}, /*ind...) while((s32[]{:T(128)}, f32[16]{0:T(128)S(1)}, ...), condition=%wide.region_2.3_spmd.clone, body=%wide.region_1.2_spmd.clone.sunk | while | flops 1048611 | bytes 5244021 | solution.py:206
  162.8 4.4 broadcast.111.clone.2
  167.1 20.9 %while.69 = (s32[]{:T(128)}, f32[16]{0:T(128)S(1)}, f32[16,128,128]{2,1,0:T(8,128)S(1)}, f32[8,16]{1,0:T(8,128)S(1)}, f32[8,16,128,128]{3,2,1,0:T(8,128)}, /*ind...) while((s32[]{:T(128)}, f32[16]{0:T(128)S(1)}, ...), condition=%wide.region_9.10_spmd.clone, body=%wide.region_8.9_spmd.clone.sunk | while | flops 1048612 | bytes 5243533 | solution.py:207
  173.4 1.6 bitcast_add_fusion.17
  189.1 1.7 copy_bitcast_fusion
  190.8 1.9 collective-permute-start.8
  193.8 1.9 collective-permute-start.7
  201.7 2.7 fusion.69
  204.4 3.3 convolution_bitcast_fusion
  207.8 2.1 slice.107
  209.9 3.2 collective-permute-start.10
  213.1 2.5 fusion.43
  215.6 4.9 convolution_bitcast_fusion.1
  220.4 2.1 slice.108
  222.6 2.1 collective-permute-start.9
  225.2 67.8 %all-reduce.3 = (f32[512]{0:T(512)S(1)}, f32[512]{0:T(512)S(1)}) all-reduce(f32[512]{0:T(512)S(1)} %dynamic-update-slice.7, f32[512]{0:T(512)S(1)} %dynamic-update-slice.8), channel_id=3, replica_groups=mesh['outer'=32,'inner'=8] {'outer'}, use_global_device_ids=true, to_apply=%add.1 | all-reduce | flops 1024 | bytes 8192
  293.1 106.8 %all-gather.10.cloned.1.call-done = f32[512,128,128]{2,1,0:T(8,128)} async-done(((f32[16,128,128]{2,1,0:T(8,128)}), f32[512,128,128]{2,1,0:T(8,128)}) %all-gather.10.cloned.1.call-update) | async-done | bytes 33554448 | tf_op jit(solution)/shard_map/all_gather | solution.py:40
  400.1 3.8 fusion.20
  403.9 5.1 fusion.26
  408.9 2.0 copy.106
  411.0 4.5 fusion.22
  415.4 2.9 fusion.25
  419.4 214.4 %all-gather.14.cloned.1.call-done = f32[512,128,128]{2,1,0:T(8,128)} async-done(((f32[16,128,128]{2,1,0:T(8,128)}), f32[512,128,128]{2,1,0:T(8,128)}) %all-gather.14.cloned.1.call-update) | async-done | bytes 33554448 | tf_op jit(solution)/shard_map/all_gather | solution.py:40
  633.9 46.6 %while.67 = (s32[]{:T(128)}, f32[16,128,128]{2,1,0:T(8,128)S(1)}, s32[]{:T(128)}, f32[32,16,128,128]{3,2,1,0:T(8,128)}, f32[32,16]{1,0:T(8,128)S(1)}, /*index=5*/s32[]{:T(128)}, s32[]{:T(128)}, s32[]{:T(128)}, s32[]{:T(128)}) while((s32[]{:T(128)}, f32[16,128,128]{2,1,0:T(8,128)S(1)}, s32[]{:T(128)}, f32[32,16,128,128]{3,2,1,0:T(8,128)}, ...), condition=%wide.region_11.12_spmd, body=%wide.region_10.11_spmd.sunk | while | flops 524294 | bytes 3146067 | solution.py:49
  680.6 3.3 convolution_bitcast_fusion.4
  684.4 3.9 convolution_bitcast_fusion.5
  689.6 6.7 scatter-add.9
  698.8 2.0 fusion.18
  702.2 5.1 scatter-add.6
  (231 shorter events, 112.5 us)
Async XLA Ops:
  7.2 155.6 %all-gather.12.cloned.1.call-start = ((), (), s32[]{:S(2)}) async-start(), calls=%async_computation.1 | async-start | bytes 9437184 | tf_op jit(solution)/shard_map/all_gather | solution.py:203
  11.1 2.3 copy-start.9
  13.3 1.0 copy-start.10
  13.3 386.6 %all-gather.10.cloned.1.call-start = ((), (), s32[]{:S(2)}) async-start(), calls=%async_computation | async-start | bytes 34603008 | tf_op jit(solution)/shard_map/all_gather | solution.py:40
  18.9 78.4 %copy-start.19 = (u32[256]{0:T(256)S(1)}, u32[256]{0:T(256)}, u32[]{:S(2)}) copy-start(u32[256]{0:T(256)} %constant.247) | copy-start | bytes 3076
  21.1 23.3 %collective-permute-start = (f32[1,16,128,128]{3,2,1,0:T(8,128)S(1)}, f32[1,16,128,128]{3,2,1,0:T(8,128)S(1)}, u32[]{:S(2)}, u32[]{:S(2)}) collective-permute-start(f32[1,16,128,128]{3,2,1,0:T(8,128)S(1)} %get-tuple-element.471), channel_id=1, source_target_pairs={{0,1},{1,2},{2,3},{3,4},{4,5},{5,6},{6,7},{7,0},{8,9},{9,10},{10,1... | collective-permute-start | bytes 3145736 | tf_op jit(solution)/shard_map/ppermute | solution.py:18
  23.8 24.1 %collective-permute-start.1 = (f32[1,16,128,128]{3,2,1,0:T(8,128)S(1)}, f32[1,16,128,128]{3,2,1,0:T(8,128)S(1)}, u32[]{:S(2)}, u32[]{:S(2)}) collective-permute-start(f32[1,16,128,128]{3,2,1,0:T(8,128)S(1)} %get-tuple-element.471), channel_id=1, source_target_pairs={{0,7},{1,0},{2,1},{3,2},{4,3},{5,4},{6,5},{7,6},{8,15},{9,8},{10,9... | collective-permute-start | bytes 3145736 | tf_op jit(solution)/shard_map/ppermute | solution.py:23
  44.4 1.0 copy-start.12
  45.4 35.1 %collective-permute-start.2 = (f32[1,16,128,128]{3,2,1,0:T(8,128)S(1)}, f32[1,16,128,128]{3,2,1,0:T(8,128)S(1)}, u32[]{:S(2)}, u32[]{:S(2)}) collective-permute-start(f32[1,16,128,128]{3,2,1,0:T(8,128)S(1)} %collective-permute-done), channel_id=1, source_target_pairs={{0,1},{1,2},{2,3},{3,4},{4,5},{5,6},{6,7},{7,0},{8,9},{9,10},{10,1... | collective-permute-start | bytes 3145736 | tf_op jit(solution)/shard_map/ppermute | solution.py:18
  47.9 32.6 %copy-start.13 = (f32[1,16,128,128]{3,2,1,0:T(8,128)}, f32[1,16,128,128]{3,2,1,0:T(8,128)S(1)}, u32[]{:S(2)}) copy-start(f32[1,16,128,128]{3,2,1,0:T(8,128)S(1)} %collective-permute-done.1) | copy-start | bytes 3145732
  47.9 35.4 %collective-permute-start.3 = (f32[1,16,128,128]{3,2,1,0:T(8,128)S(1)}, f32[1,16,128,128]{3,2,1,0:T(8,128)}, u32[]{:S(2)}, u32[]{:S(2)}) collective-permute-start(f32[1,16,128,128]{3,2,1,0:T(8,128)S(1)} %collective-permute-done.1), channel_id=1, source_target_pairs={{0,7},{1,0},{2,1},{3,2},{4,3},{5,4},{6,5},{7,6},{8,15},{9,8},{10,9... | collective-permute-start | bytes 3145736 | tf_op jit(solution)/shard_map/ppermute | solution.py:23
  80.5 2.8 copy-start.15
  80.5 14.2 %collective-permute-start.4 = (f32[1,16,128,128]{3,2,1,0:T(8,128)S(1)}, f32[1,16,128,128]{3,2,1,0:T(8,128)}, u32[]{:S(2)}, u32[]{:S(2)}) collective-permute-start(f32[1,16,128,128]{3,2,1,0:T(8,128)S(1)} %collective-permute-done.2), channel_id=1, source_target_pairs={{0,1},{1,2},{2,3},{3,4},{4,5},{5,6},{6,7},{7,0},{8,9},{9,10},{10,1... | collective-permute-start | bytes 3145736 | tf_op jit(solution)/shard_map/ppermute | solution.py:18
  83.2 48.9 %collective-permute-start.5 = (f32[1,16,128,128]{3,2,1,0:T(8,128)}, f32[1,16,128,128]{3,2,1,0:T(8,128)}, u32[]{:S(2)}, u32[]{:S(2)}) collective-permute-start(f32[1,16,128,128]{3,2,1,0:T(8,128)} %collective-permute-done.3), channel_id=1, source_target_pairs={{0,7},{1,0},{2,1},{3,2},{4,3},{5,4},{6,5},{7,6},{8,15},{9,8},{10,9... | collective-permute-start | bytes 3145736 | tf_op jit(solution)/shard_map/ppermute | solution.py:23
  94.7 39.8 %collective-permute-start.6 = (f32[1,16,128,128]{3,2,1,0:T(8,128)}, f32[1,16,128,128]{3,2,1,0:T(8,128)}, u32[]{:S(2)}, u32[]{:S(2)}) collective-permute-start(f32[1,16,128,128]{3,2,1,0:T(8,128)} %collective-permute-done.4), channel_id=1, source_target_pairs={{0,1},{1,2},{2,3},{3,4},{4,5},{5,6},{6,7},{7,0},{8,9},{9,10},{10,1... | collective-permute-start | bytes 3145736 | tf_op jit(solution)/shard_map/ppermute | solution.py:18
  122.4 2.5 copy-start.14
  124.8 1.6 copy-start.16
  161.6 1.0 copy-start
  162.7 471.1 %all-gather.14.cloned.1.call-start = ((), (), s32[]{:S(2)}) async-start(), calls=%async_computation.2 | async-start | bytes 34603008 | tf_op jit(solution)/shard_map/all_gather | solution.py:40
  188.0 1.0 copy-start.1
  189.1 7.2 %copy-start.18 = (u32[256]{0:T(256)S(1)}, u32[256]{0:T(256)}, u32[]{:S(2)}) copy-start(u32[256]{0:T(256)} %constant.252) | copy-start | bytes 3076
  190.8 10.9 %collective-permute-start.8 = (bf16[64,16,128]{2,0,1:T(8,128)(2,1)}, bf16[64,16,128]{2,0,1:T(8,128)(2,1)}, u32[]{:S(2)}, u32[]{:S(2)}) collective-permute-start(bf16[64,16,128]{2,0,1:T(8,128)(2,1)} %copy_bitcast_fusion), channel_id=1, source_target_pairs={{0,1},{1,2},{2,3},{3,4},{4,5},{5,6},{6,7},{7,8},{8,9},{9,10},{10,1... | collective-permute-start | bytes 786440 | tf_op jit(solution)/shard_map/ppermute | solution.py:33
  193.8 19.3 %collective-permute-start.7 = (bf16[64,16,128]{2,0,1:T(8,128)(2,1)S(1)}, bf16[64,16,128]{2,0,1:T(8,128)(2,1)}, u32[]{:S(2)}, u32[]{:S(2)}) collective-permute-start(bf16[64,16,128]{2,0,1:T(8,128)(2,1)S(1)} %copy_bitcast_fusion.1), channel_id=1, source_target_pairs={{0,1},{1,2},{2,3},{3,4},{4,5},{5,6},{6,7},{7,8},{8,9},{9,10},{10,1... | collective-permute-start | bytes 786440 | tf_op jit(solution)/shard_map/ppermute | solution.py:33
  196.0 8.5 %copy-start.17 = (bf16[128,16,128]{2,0,1:T(8,128)(2,1)}, bf16[128,16,128]{2,0,1:T(8,128)(2,1)S(1)}, u32[]{:S(2)}) copy-start(bf16[128,16,128]{2,0,1:T(8,128)(2,1)S(1)} %copy.84) | copy-start | bytes 1572868
  196.3 16.8 %copy-start.4 = (bf16[128,16,128]{2,0,1:T(8,128)(2,1)}, bf16[128,16,128]{2,0,1:T(8,128)(2,1)S(1)}, u32[]{:S(2)}) copy-start(bf16[128,16,128]{2,0,1:T(8,128)(2,1)S(1)} %copy.82) | copy-start | bytes 1572868
  198.2 2.0 copy-start.7
  198.8 2.9 copy-start.5
  209.9 478.3 %collective-permute-start.10 = (bf16[64,16,128]{0,2,1:T(8,128)(2,1)}, bf16[64,16,128]{0,2,1:T(8,128)(2,1)}, u32[]{:S(2)}, u32[]{:S(2)}) collective-permute-start(bf16[64,16,128]{0,2,1:T(8,128)(2,1)} %slice.107), channel_id=1, source_target_pairs={{1,0},{2,1},{3,2},{4,3},{5,4},{6,5},{7,6},{8,7},{9,8},{10,9},{11,1... | collective-permute-start | bytes 786440 | tf_op jit(solution)/shard_map/ppermute | solution.py:33
  222.6 478.2 %collective-permute-start.9 = (bf16[64,16,128]{0,2,1:T(8,128)(2,1)}, bf16[64,16,128]{0,2,1:T(8,128)(2,1)}, u32[]{:S(2)}, u32[]{:S(2)}) collective-permute-start(bf16[64,16,128]{0,2,1:T(8,128)(2,1)} %slice.108), channel_id=1, source_target_pairs={{1,0},{2,1},{3,2},{4,3},{5,4},{6,5},{7,6},{8,7},{9,8},{10,9},{11,1... | collective-permute-start | bytes 786440 | tf_op jit(solution)/shard_map/ppermute | solution.py:33
  680.6 3.4 copy-start.8
  680.6 3.4 copy-start.11
  684.4 3.9 copy-start.2
  696.3 2.5 copy-start.3
  696.3 2.5 copy-start.6
Sparse Core Ops, SparseCore 0:
  13.5 70.7 all-gather.11
  162.8 237.1 all-gather.9
  402.5 231.2 all-gather.13
